TPU v7x, 32 devices: a whole 2x2x4 slice. The times are simulated.
32 devices in a mesh: dp: 8 (over y, x, core), tensor: 4 (over z).
Axes of the slice: x: 2, y: 2, z: 4, core: 2. Of those that a mesh axis runs over, the one named last changes fastest.
Arguments:
- tokens: bfloat16 [8192, 2048], P(('dp', 'tensor')), may hold values from -6 to 6
- lengths: int32 [8], P('dp'), may hold values from 256 to 1024, as said below
- ln1_gain: bfloat16 [2048], P('dp'), may hold values from 0.5 to 1.5
- ln1_bias: bfloat16 [2048], P('dp'), may hold values from -4 to 4
- qkv_weight: bfloat16 [2048, 3, 2048], P('dp', None, 'tensor'), may hold values from -0.125 to 0.125
- qv_bias: bfloat16 [2, 16, 128], P(None, 'tensor', 'dp'), may hold values from -4 to 4
- out_weight: bfloat16 [2048, 2048], P('tensor', 'dp'), may hold values from -0.75 to 0.75
- out_bias: bfloat16 [2048], P('dp'), may hold values from -4 to 4
- ln2_gain: bfloat16 [2048], P('dp'), may hold values from 0.5 to 1.5
- ln2_bias: bfloat16 [2048], P('dp'), may hold values from -4 to 4
- up_weight: bfloat16 [2048, 8192], P('dp', 'tensor'), may hold values from -0.125 to 0.125
- up_bias: bfloat16 [512, 16], P('tensor', 'dp'), may hold values from -4 to 4
- down_weight: bfloat16 [8192, 2048], P('tensor', 'dp'), may hold values from -0.0625 to 0.0625
- down_bias: bfloat16 [2048], P('dp'), may hold values from -4 to 4
- cotangent: bfloat16 [8192, 2048], P(('dp', 'tensor')), may hold values from -6 to 6
Outputs:
- output: bfloat16 [8192, 2048], P(('dp', 'tensor'))
- tokens_grad: float32 [8192, 2048], P(('dp', 'tensor'))
- ln1_gain_grad: float32 [2048], P('dp')
- ln1_bias_grad: float32 [2048], P('dp')
- qkv_weight_grad: float32 [2048, 3, 2048], P('dp', None, 'tensor')
- qv_bias_grad: float32 [2, 16, 128], P(None, 'tensor', 'dp')
- out_weight_grad: float32 [2048, 2048], P('tensor', 'dp')
- out_bias_grad: float32 [2048], P('dp')
- ln2_gain_grad: float32 [2048], P('dp')
- ln2_bias_grad: float32 [2048], P('dp')
- up_weight_grad: float32 [2048, 8192], P('dp', 'tensor')
- up_bias_grad: float32 [512, 16], P('tensor', 'dp')
- down_weight_grad: float32 [8192, 2048], P('tensor', 'dp')
- down_bias_grad: float32 [2048], P('dp')
- stream_rms: float32 [5], replicated
Inputs may be any that keep to these rules, and one draw needn't show every extreme that they name: `lengths`: each sequence's true token count.
All inputs are finite; a program needn't handle non-finite values.
Results may differ from a plain program's by a relative error of at most 0.02.
Values may be sent and summed in bfloat16 or wider, within the bound.
A program may use at most 256 MiB of HBM per device.

v0:
```python
import jax
import jax.numpy as jnp
from jax import lax
from jax.sharding import PartitionSpec as P

D = 2048
HD = 128
LEN = 1024
EPS = 1e-05


def layer_norm(values, norm_gain, norm_shift):
    center = values - jnp.mean(values, axis=-1, keepdims=True)
    spread = lax.rsqrt(jnp.mean(center * center, axis=-1, keepdims=True) + EPS)
    normed = center * spread
    return (normed * norm_gain + norm_shift, normed, spread)


def norm_backward(upstream, normed, spread, norm_gain):
    scaled = upstream * norm_gain
    mean_part = jnp.mean(scaled, axis=-1, keepdims=True)
    across = jnp.mean(scaled * normed, axis=-1, keepdims=True)
    return spread * (scaled - mean_part - normed * across)


def gelu_tanh(values):
    return jax.nn.gelu(values, approximate=True)


def contract_rows(left, right):
    return lax.dot_general(
        left, right, (((0,), (0,)), ((), ())), preferred_element_type=jnp.float32
    )


def contract_cols(left, right):
    return lax.dot_general(
        left, right, (((1,), (1,)), ((), ())), preferred_element_type=jnp.float32
    )


def allowed_keys(first_row, block_size, positions, length):
    query_pos = first_row + jnp.arange(block_size, dtype=jnp.int32)
    return (positions[None, :] <= query_pos[:, None]) & (positions[None, :] < length)


def attend_forward(queries, key_rows, value_rows, length):
    block_size = min(512, LEN)
    positions = jnp.arange(LEN, dtype=jnp.int32)
    score_scale = HD ** (-0.5)

    def one_block(block_index):
        first_row = block_index * block_size
        query_block = lax.dynamic_slice_in_dim(queries, first_row, block_size, 0)
        scores = (
            jnp.einsum("qhd,khd->hqk", query_block, key_rows, preferred_element_type=jnp.float32)
            * score_scale
        )
        allowed = allowed_keys(first_row, block_size, positions, length)
        scores = jnp.where(allowed[None], scores, -1e30)
        row_max = jnp.max(scores, axis=-1, keepdims=True)
        powers = jnp.exp(scores - row_max)
        totals = jnp.sum(powers, axis=-1, keepdims=True)
        shares = (powers / totals).astype(jnp.bfloat16)
        mixed = jnp.einsum("hqk,khd->qhd", shares, value_rows, preferred_element_type=jnp.float32)
        return (mixed.astype(jnp.bfloat16), (row_max + jnp.log(totals))[..., 0])

    mixed, log_totals = lax.map(one_block, jnp.arange(LEN // block_size, dtype=jnp.int32))
    return (mixed.reshape(LEN, queries.shape[1], HD), log_totals)


def attend_backward(queries, key_rows, value_rows, grad_out, log_totals, length):
    block_size = min(512, LEN)
    positions = jnp.arange(LEN, dtype=jnp.int32)
    score_scale = HD ** (-0.5)

    def one_block(carry, block_index):
        key_grad, value_grad = carry
        first_row = block_index * block_size
        query_block = lax.dynamic_slice_in_dim(queries, first_row, block_size, 0)
        grad_block = lax.dynamic_slice_in_dim(grad_out, first_row, block_size, 0)
        scores = (
            jnp.einsum("qhd,khd->hqk", query_block, key_rows, preferred_element_type=jnp.float32)
            * score_scale
        )
        allowed = allowed_keys(first_row, block_size, positions, length)
        shares = jnp.where(allowed[None], jnp.exp(scores - log_totals[block_index][..., None]), 0.0)
        value_grad = value_grad + jnp.einsum(
            "hqk,qhd->khd",
            shares.astype(jnp.bfloat16),
            grad_block,
            preferred_element_type=jnp.float32,
        )
        share_grad = jnp.einsum(
            "qhd,khd->hqk", grad_block, value_rows, preferred_element_type=jnp.float32
        )
        centre = jnp.sum(shares * share_grad, axis=-1, keepdims=True)
        score_grad = (shares * (share_grad - centre)).astype(jnp.bfloat16)
        query_grad = (
            jnp.einsum("hqk,khd->qhd", score_grad, key_rows, preferred_element_type=jnp.float32)
            * score_scale
        )
        key_grad = (
            key_grad
            + jnp.einsum(
                "hqk,qhd->khd", score_grad, query_block, preferred_element_type=jnp.float32
            )
            * score_scale
        )
        return ((key_grad, value_grad), query_grad.astype(jnp.bfloat16))

    zeros_kv = jnp.zeros((LEN, queries.shape[1], HD), jnp.float32)
    (key_grad, value_grad), query_grads = lax.scan(
        one_block, (zeros_kv, zeros_kv), jnp.arange(LEN // block_size, dtype=jnp.int32)
    )
    return (
        query_grads.reshape(LEN, queries.shape[1], HD),
        key_grad.astype(jnp.bfloat16),
        value_grad.astype(jnp.bfloat16),
    )


def shards(
    tokens,
    lengths,
    ln1_gain,
    ln1_bias,
    qkv_weight,
    qv_bias,
    out_weight,
    out_bias,
    ln2_gain,
    ln2_bias,
    up_weight,
    up_bias,
    down_weight,
    down_bias,
    cotangent,
):
    (
        gain_one,
        shift_one,
        qkv_full,
        qv_full,
        out_full,
        out_shift,
        gain_two,
        shift_two,
        up_full,
        up_shift,
        down_full,
        down_shift,
    ) = (
        lax.all_gather(ln1_gain, "dp", axis=0, tiled=True),
        lax.all_gather(ln1_bias, "dp", axis=0, tiled=True),
        lax.all_gather(qkv_weight, "dp", axis=0, tiled=True),
        lax.all_gather(qv_bias, "dp", axis=2, tiled=True),
        lax.all_gather(out_weight, "dp", axis=1, tiled=True),
        lax.all_gather(out_bias, "dp", axis=0, tiled=True),
        lax.all_gather(ln2_gain, "dp", axis=0, tiled=True),
        lax.all_gather(ln2_bias, "dp", axis=0, tiled=True),
        lax.all_gather(up_weight, "dp", axis=0, tiled=True),
        lax.all_gather(up_bias, "dp", axis=1, tiled=True),
        lax.all_gather(down_weight, "dp", axis=1, tiled=True),
        lax.all_gather(down_bias, "dp", axis=0, tiled=True),
    )
    gain_one = gain_one.astype(jnp.float32)
    shift_one = shift_one.astype(jnp.float32)
    gain_two = gain_two.astype(jnp.float32)
    shift_two = shift_two.astype(jnp.float32)
    out_shift = out_shift.astype(jnp.float32)
    down_shift = down_shift.astype(jnp.float32)
    own_rows = tokens.shape[0]
    group_rows = own_rows * lax.axis_size("tensor")
    seq_count = lengths.shape[0]
    local_heads = qkv_full.shape[2] // HD
    local_width = qkv_full.shape[2]
    local_hidden = up_full.shape[1]
    own_first = lax.axis_index("tensor") * own_rows
    positions = jnp.arange(group_rows, dtype=jnp.int32)
    seq_ids = positions // LEN
    length_rows = jnp.sum(
        jnp.where(
            seq_ids[:, None] == jnp.arange(seq_count, dtype=jnp.int32)[None, :], lengths[None, :], 0
        ),
        axis=1,
    )
    valid_all = (positions % LEN < length_rows).astype(jnp.float32)[:, None]
    valid_own = lax.dynamic_slice_in_dim(valid_all, own_first, own_rows, 0)
    own_count = jnp.sum(valid_own)
    tokens_in, cotangent_in = (
        lax.all_gather(tokens, "tensor", axis=0, tiled=True),
        lax.all_gather(cotangent, "tensor", axis=0, tiled=True),
    )

    def own_part(values):
        return lax.dynamic_slice_in_dim(values, own_first, own_rows, 0)

    def branch_total(source, weight):
        return lax.psum(
            jnp.dot(source, weight, preferred_element_type=jnp.float32).astype(jnp.bfloat16),
            "tensor",
        ).astype(jnp.float32)

    def input_total(source, weight):
        return lax.psum(contract_cols(source, weight).astype(jnp.bfloat16), "tensor").astype(
            jnp.float32
        )

    recorded = []

    def record(values):
        mine = own_part(values)
        square_sum = jnp.sum(valid_own * mine * mine)
        recorded.append(lax.psum((square_sum, own_count), ("dp", "tensor")))

    x_values = tokens_in.astype(jnp.float32)
    record(x_values)
    ln1_out, normed_one, spread_one = layer_norm(x_values, gain_one, shift_one)
    normed_a = ln1_out.astype(jnp.bfloat16)
    qkv_flat = qkv_full.reshape(D, 3 * local_width)
    projected = jnp.dot(normed_a, qkv_flat, preferred_element_type=jnp.float32)
    qv_values = qv_full.astype(jnp.float32)
    bias_all = jnp.stack([qv_values[0], jnp.zeros_like(qv_values[0]), qv_values[1]]).reshape(
        3 * local_width
    )
    qkv_low = (projected + bias_all).astype(jnp.bfloat16)
    qkv_seq = qkv_low.reshape(seq_count, LEN, 3, local_heads, HD)

    def forward_sequence(pair):
        seq_qkv, seq_len = pair
        return attend_forward(seq_qkv[:, 0], seq_qkv[:, 1], seq_qkv[:, 2], seq_len)

    attended, log_totals = lax.map(forward_sequence, (qkv_seq, lengths))
    attended_rows = attended.reshape(group_rows, local_width)
    attn_out = branch_total(attended_rows, out_full) + out_shift
    record(attn_out)
    middle = x_values + attn_out
    record(middle)
    ln2_out, normed_two, spread_two = layer_norm(middle, gain_two, shift_two)
    normed_c = ln2_out.astype(jnp.bfloat16)
    hidden_pre = jnp.dot(normed_c, up_full, preferred_element_type=jnp.float32) + up_shift.astype(
        jnp.float32
    ).reshape(local_hidden)
    hidden_act = gelu_tanh(hidden_pre).astype(jnp.bfloat16)
    mlp_out = branch_total(hidden_act, down_full) + down_shift
    record(mlp_out)
    result = middle + mlp_out
    record(result)
    grad_y = cotangent_in.astype(jnp.float32) * valid_all
    down_bias_grad = jnp.sum(own_part(grad_y), axis=0)
    grad_m = grad_y.astype(jnp.bfloat16)
    down_weight_grad = contract_rows(hidden_act, grad_m)
    grad_act = contract_cols(grad_m, down_full)
    gelu_value, gelu_back = jax.vjp(gelu_tanh, hidden_pre)
    grad_u = gelu_back(grad_act)[0].astype(jnp.bfloat16)
    up_bias_grad = jnp.sum(grad_u, axis=0, dtype=jnp.float32).reshape(local_hidden // 16, 16)
    up_weight_grad = contract_rows(normed_c, grad_u)
    grad_c = input_total(grad_u, up_full)
    grad_mid = grad_y + norm_backward(grad_c, normed_two, spread_two, gain_two)
    ln2_gain_grad = jnp.sum(own_part(grad_c * normed_two), axis=0)
    ln2_bias_grad = jnp.sum(own_part(grad_c), axis=0)
    out_bias_grad = jnp.sum(own_part(grad_mid), axis=0)
    grad_z = grad_mid.astype(jnp.bfloat16)
    out_weight_grad = contract_rows(attended_rows, grad_z)
    grad_o = contract_cols(grad_z, out_full).astype(jnp.bfloat16)
    grad_o_seq = grad_o.reshape(seq_count, LEN, local_heads, HD)

    def backward_sequence(group):
        seq_qkv, seq_grad, seq_totals, seq_len = group
        return attend_backward(
            seq_qkv[:, 0], seq_qkv[:, 1], seq_qkv[:, 2], seq_grad, seq_totals, seq_len
        )

    grad_q, grad_k, grad_v = lax.map(backward_sequence, (qkv_seq, grad_o_seq, log_totals, lengths))
    grad_qkv = jnp.stack([grad_q, grad_k, grad_v], axis=2).reshape(group_rows, 3 * local_width)
    qv_bias_grad = jnp.stack(
        [
            jnp.sum(grad_q, axis=(0, 1), dtype=jnp.float32),
            jnp.sum(grad_v, axis=(0, 1), dtype=jnp.float32),
        ]
    )
    qkv_weight_grad = contract_rows(normed_a, grad_qkv).reshape(D, 3, local_width)
    grad_a = input_total(grad_qkv, qkv_flat)
    grad_x_all = grad_mid + norm_backward(grad_a, normed_one, spread_one, gain_one)
    tokens_grad = own_part(grad_x_all)
    ln1_gain_grad = jnp.sum(own_part(grad_a * normed_one), axis=0)
    ln1_bias_grad = jnp.sum(own_part(grad_a), axis=0)
    (
        qkv_weight_out,
        qv_bias_out,
        out_weight_out,
        up_weight_out,
        up_bias_out,
        down_weight_out,
        ln1_gain_part,
        ln1_bias_part,
        out_bias_part,
        ln2_gain_part,
        ln2_bias_part,
        down_bias_part,
    ) = (
        lax.psum_scatter(
            qkv_weight_grad.astype(jnp.bfloat16), "dp", scatter_dimension=0, tiled=True
        ).astype(jnp.float32),
        lax.psum_scatter(
            qv_bias_grad.astype(jnp.bfloat16), "dp", scatter_dimension=2, tiled=True
        ).astype(jnp.float32),
        lax.psum_scatter(
            out_weight_grad.astype(jnp.bfloat16), "dp", scatter_dimension=1, tiled=True
        ).astype(jnp.float32),
        lax.psum_scatter(
            up_weight_grad.astype(jnp.bfloat16), "dp", scatter_dimension=0, tiled=True
        ).astype(jnp.float32),
        lax.psum_scatter(
            up_bias_grad.astype(jnp.bfloat16), "dp", scatter_dimension=1, tiled=True
        ).astype(jnp.float32),
        lax.psum_scatter(
            down_weight_grad.astype(jnp.bfloat16), "dp", scatter_dimension=1, tiled=True
        ).astype(jnp.float32),
        lax.psum_scatter(
            ln1_gain_grad.astype(jnp.bfloat16), "dp", scatter_dimension=0, tiled=True
        ).astype(jnp.float32),
        lax.psum_scatter(
            ln1_bias_grad.astype(jnp.bfloat16), "dp", scatter_dimension=0, tiled=True
        ).astype(jnp.float32),
        lax.psum_scatter(
            out_bias_grad.astype(jnp.bfloat16), "dp", scatter_dimension=0, tiled=True
        ).astype(jnp.float32),
        lax.psum_scatter(
            ln2_gain_grad.astype(jnp.bfloat16), "dp", scatter_dimension=0, tiled=True
        ).astype(jnp.float32),
        lax.psum_scatter(
            ln2_bias_grad.astype(jnp.bfloat16), "dp", scatter_dimension=0, tiled=True
        ).astype(jnp.float32),
        lax.psum_scatter(
            down_bias_grad.astype(jnp.bfloat16), "dp", scatter_dimension=0, tiled=True
        ).astype(jnp.float32),
    )
    ln1_gain_out, ln1_bias_out, out_bias_out, ln2_gain_out, ln2_bias_out, down_bias_out = lax.psum(
        (ln1_gain_part, ln1_bias_part, out_bias_part, ln2_gain_part, ln2_bias_part, down_bias_part),
        "tensor",
    )
    totals = jnp.stack([entry[0] for entry in recorded])
    count = recorded[0][1]
    stream_rms = jnp.sqrt(totals / (count * D))
    return (
        own_part(result).astype(jnp.bfloat16),
        tokens_grad,
        ln1_gain_out,
        ln1_bias_out,
        qkv_weight_out,
        qv_bias_out,
        out_weight_out,
        out_bias_out,
        ln2_gain_out,
        ln2_bias_out,
        up_weight_out,
        up_bias_out,
        down_weight_out,
        down_bias_out,
        stream_rms,
    )


def solution(mesh):
    placed = (
        P(("dp", "tensor"), None),
        P("dp"),
        P("dp"),
        P("dp"),
        P("dp", None, "tensor"),
        P(None, "tensor", "dp"),
        P("tensor", "dp"),
        P("dp"),
        P("dp"),
        P("dp"),
        P("dp", "tensor"),
        P("tensor", "dp"),
        P("tensor", "dp"),
        P("dp"),
        P(("dp", "tensor"), None),
    )
    return jax.shard_map(
        shards,
        mesh=mesh,
        in_specs=placed,
        out_specs=(
            P(("dp", "tensor"), None),
            P(("dp", "tensor"), None),
            P("dp"),
            P("dp"),
            P("dp", None, "tensor"),
            P(None, "tensor", "dp"),
            P("tensor", "dp"),
            P("dp"),
            P("dp"),
            P("dp"),
            P("dp", "tensor"),
            P("tensor", "dp"),
            P("tensor", "dp"),
            P("dp"),
            P(),
        ),
        check_vma=False,
    )
```

profile of v0, /device:TPU:0, one launch (start us, length us, event | category | flops | bytes accessed | tf_op | source)
XLA Modules:
  0.0 1390.4 jit_solution(11187329936646952826)
XLA Ops:
  12.4 10.4 all-gather.1
  22.8 8.9 all-gather
  32.5 8.3 all_gather.46
  41.2 51.9 %all-gather.14.cloned.1.call-done = bf16[1024,2048]{1,0:T(8,128)(2,1)} async-done(((bf16[256,2048]{1,0:T(8,128)(2,1)}), bf16[1024,2048]{1,0:T(8,128)(2,1)}) %all-gather.14.cloned.1.call-update) | async-done | bytes 4194320 | tf_op jit(solution)/shard_map/all_gather | solution.py:192
  99.3 41.3 %all-gather.16.cloned.1.call-done = bf16[2048,3,512]{0,2,1:T(8,128)(2,1)} async-done(((bf16[256,3,512]{0,2,1:T(8,128)(2,1)}), bf16[2048,3,512]{0,2,1:T(8,128)(2,1)}) %all-gather.16.cloned.1.call-update) | async-done | bytes 6291472 | tf_op jit(solution)/shard_map/all_gather | solution.py:156
  140.6 12.5 add_convert_fusion.2
  153.1 6.3 squeeze.48
  162.8 22.4 %while.50 = (s32[]{:T(128)}, bf16[2,512,4,128]{3,2,1,0:T(4,128)(2,1)}, f32[2,4,512]{2,1,0:T(4,128)S(1)}, s32[2]{0:T(128)S(1)}, s32[]{:T(128)}, /*index=5*/bf16[1...) while((s32[]{:T(128)}, ...), condition=%wide.region_5.6_spmd.clone.clone, body=%wide.region_2.5_spmd.clone.clone.sunk | while | flops 1100217856 | bytes 39917828 | solution.py:68
  185.3 7.0 convolution_convert_fusion.6
  195.1 8.8 all-gather.4
  203.9 8.1 all-gather.3
  212.0 8.8 all-gather.2
  220.8 8.0 all-gather.5
  229.0 118.4 %all-reduce.15.cloned.1.call-done = bf16[1024,2048]{1,0:T(8,128)(2,1)} async-done(((bf16[1024,2048]{1,0:T(8,128)(2,1)}), bf16[1024,2048]{1,0:T(8,128)(2,1)}) %all-reduce.15.cloned.1.call-update) | async-done | bytes 4194320 | tf_op jit(solution)/shard_map/psum | solution.py:200
  347.4 11.2 fusion.84
  358.6 4.5 multiply_reduce_fusion.3
  368.3 34.0 %all-gather.20.cloned.1.call-done = bf16[2048,2048]{1,0:T(8,128)(2,1)} async-done(((bf16[256,2048]{1,0:T(8,128)(2,1)}), bf16[2048,2048]{1,0:T(8,128)(2,1)}) %all-gather.20.cloned.1.call-update) | async-done | bytes 8388624 | tf_op jit(solution)/shard_map/all_gather | solution.py:162
  402.4 15.9 %fusion.69 = f32[1024,2048]{1,0:T(8,128)} fusion(bf16[2048,2048]{1,0:T(8,128)(2,1)} %all-gather.20.cloned.1.call-done, f32[1024,2048]{1,0:T(8,128)} %subtract_multiply_fusion, f32[2048]{0:T(1024)S(1)} %bitcast.153, f32[2048]{0:T(1024)S(1)} %bitcast.140), kind=kOutput, calls=%fused_computation.120 | convolution fusion | flops 8596226048 | bytes 25182208 | tf_op jit(solution)/shard_map/dot_general | solution.py:242
  418.3 66.3 %all-gather.24.cloned.1.call-done = bf16[1024,2048]{1,0:T(8,128)(2,1)} async-done(((bf16[256,2048]{1,0:T(8,128)(2,1)}), bf16[1024,2048]{1,0:T(8,128)(2,1)}) %all-gather.24.cloned.1.call-update) | async-done | bytes 4194320 | tf_op jit(solution)/shard_map/all_gather | solution.py:193
  484.6 56.3 %all-gather.22.cloned.1.call-done = bf16[2048,2048]{1,0:T(8,128)(2,1)} async-done(((bf16[2048,256]{1,0:T(8,128)(2,1)}), bf16[2048,2048]{1,0:T(8,128)(2,1)}) %all-gather.22.cloned.1.call-update) | async-done | bytes 8388624 | tf_op jit(solution)/shard_map/all_gather | solution.py:164
  540.8 19.2 %fusion.87 = (bf16[2048]{0:T(1024)(128)(2,1)}, bf16[1024,2048]{1,0:T(8,128)(2,1)S(1)}) fusion(f32[1024,2048]{1,0:T(8,128)} %fusion.69, f32[2048]{0:T(1024)S(1)} %reshape.277, bf16[2048,2048]{1,0:T(8,128)(2,1)} %all-gather.22.cloned.1.call-done, f32[1024]{0:T(1024)S(1)} %fusion.82, bf16[1024,2048]{1,0:T(8,128)(2,1)} %all-gather.24.cloned.1.call-done), kind=kOutput, calls=%fused_computation.167 | convolution fusion | flops 8642361344 | bytes 25182208 | tf_op jit(solution)/shard_map/dot_general | solution.py:37
  562.1 13.1 convolution_convert_fusion.4
  575.3 155.1 %all-reduce.17.cloned.1.call-done = bf16[1024,2048]{1,0:T(8,128)(2,1)} async-done(((bf16[1024,2048]{1,0:T(8,128)(2,1)}), bf16[1024,2048]{1,0:T(8,128)(2,1)}) %all-reduce.17.cloned.1.call-update) | async-done | bytes 4194320 | tf_op jit(solution)/shard_map/psum | solution.py:206
  730.4 6.0 multiply_reduce_fusion.5
  737.5 8.4 convert_multiply_fusion
  745.8 6.5 fusion.66
  752.4 41.1 %while.51 = (s32[]{:T(128)}, f32[1024,4,128]{0,2,1:T(8,128)S(1)}, f32[1024,4,128]{0,2,1:T(8,128)}, bf16[2,512,4,128]{3,1,2,0:T(8,128)(2,1)}, s32[2]{0:T(128)S(1)...) while((s32[]{:T(128)}, f32[1024,4,128]{0,2,1:T(8,128)S(1)}, ...), condition=%wide.region_15.16_spmd.clone.clone, body=%wide.region_13.15_spmd.clone.clone.sunk | while | flops 2720005632 | bytes 100202928 | solution.py:113
  763.0 4.0 multiply_reduce_fusion.8
  779.1 5.1 bitcast_add_fusion.5
  784.2 4.0 multiply_reduce_fusion.8
  797.8 7.4 convolution_convert_fusion.7
  805.3 16.3 %convolution_convert_fusion.5 = bf16[1024,2048]{1,0:T(8,128)(2,1)} fusion(bf16[2048,2048]{1,0:T(8,128)(2,1)} %all-gather.22.cloned.1.call-done, f32[1024,2048]{1,0:T(8,128)} %fusion.69, f32[2048]{0:T(1024)S(1)} %copy-done.27), kind=kOutput, calls=%fused_computation.86 | convolution fusion | flops 8613003264 | bytes 20979712 | tf_op jit(solution)/shard_map/dot_general | solution.py:201
  827.6 4.7 copy.114
  832.3 11.2 convolution_convert_fusion.3
  844.2 20.2 %convolution_convert_fusion = bf16[2048,2048]{1,0:T(8,128)(2,1)} fusion(bf16[1024,2048]{1,0:T(8,128)(2,1)} %all-gather.24.cloned.1.call-done, f32[1024]{0:T(1024)S(1)} %copy-done.25, f32[1024,2048]{1,0:T(8,128)} %fusion.69, f32[2048]{0:T(1024)S(1)} %copy-done.27), kind=kOutput, calls=%fused_computation.77 | convolution fusion | flops 8621391872 | bytes 20983808 | tf_op jit(solution)/shard_map/dot_general | solution.py:31
  865.1 14.8 %convolution_convert_fusion.1 = bf16[2048,2048]{1,0:T(8,128)(2,1)} fusion(bf16[1024,2048]{1,0:T(8,128)(2,1)} %copy-done.39, f32[1024,2048]{1,0:T(8,128)} %subtract_multiply_fusion, f32[2048]{0:T(1024)S(1)} %bitcast.154, f32[2048]{0:T(1024)S(1)} %bitcast.143), kind=kOutput, calls=%fused_computation.78 | convolution fusion | flops 8600420352 | bytes 20987904 | tf_op jit(solution)/shard_map/dot_general | solution.py:31
  880.6 14.2 %convolution_convert_fusion.2 = bf16[2048,3,512]{2,0,1:T(8,128)(2,1)} fusion(bf16[3,512,1024]{2,1,0:T(8,128)(2,1)} %bitcast.135, f32[2048]{0:T(1024)S(1)} %bitcast.152, f32[2048]{0:T(1024)S(1)} %bitcast.145, bf16[1024,2048]{1,0:T(8,128)(2,1)} %all-gather.14.cloned.1.call-done, f32[1024]{0:T(1024)S(1)} %copy-done.23, f32[1024]{0:T(1024)S(1)} %copy-done.19), kind=kOutput, calls=%fused_computation.81 | convolution fusion | flops 6458179584 | bytes 13656064 | tf_op jit(solution)/shard_map/dot_general | solution.py:31
  896.7 9.1 all-gather.6
  906.6 6.5 convert_element_type.197
  923.4 243.2 %all-reduce.19.cloned.1.call-done = (bf16[1024,2048]{1,0:T(8,128)(2,1)}, bf16[1024,2048]{1,0:T(8,128)(2,1)}) async-done(((bf16[1024,2048]{1,0:T(8,128)(2,1)}, bf16[1024,2048]{1,0:T(8,128)(2,1)}), (bf16[1024,2048]{1,0:T(8,128)(2,1)}, bf16[1024,2048]{1,0:T(8,128)(2,1)})) %all-reduce.19.cloned.1.call-update) | async-done | bytes 8388624 | tf_op jit(solution)/shard_map/psum | solution.py:200
  1170.0 5.6 fusion.52
  1175.6 40.5 %all-reduce.7 = (f32[1]{0:T(128)}, f32[1]{0:T(128)}, f32[1]{0:T(128)}, f32[1]{0:T(128)}, f32[1]{0:T(128)}, /*index=5*/f32[]{:T(128)}) all-reduce(f32[1]{0:T(128)} %bitcast.25, f32[1]{0:T(128)} %bitcast.26, f32[1]{0:T(128)} %bitcast.27, f32[1]{0:T(128)} %bitcast.28, ...), channel_id=1, replica_groups=mesh['dp'=8,'tensor'=4] {'dp','tensor'}, use_global_device_ids=true, to_apply=%region_47.48 | all-reduce | flops 6 | bytes 48 | tf_op jit(solution)/shard_map/psum | solution.py:215
  1216.1 6.7 convert_element_type.225
  1225.8 4.8 dynamic-slice_reduce_fusion.3
  1230.6 24.5 %all-reduce.9 = (bf16[2048]{0:T(1024)(128)(2,1)S(1)}, bf16[2048]{0:T(1024)(128)(2,1)S(1)}, bf16[2048]{0:T(1024)(128)(2,1)S(1)}, bf16[2048]{0:T(1024)(128)(2,1)S(...) all-reduce(bf16[2048]{0:T(1024)(128)(2,1)S(1)} %get-tuple-element.5, ...), channel_id=2, replica_groups=mesh['dp'=8,'tensor'=4] {'dp'}, use_global_device_ids=true, to_apply=%region_20.21.clone | all-reduce | flops 14336 | bytes 57344
  1262.7 53.5 %reduce-scatter.13.cloned.1.call-done = bf16[256,2048]{1,0:T(8,128)(2,1)} async-done(((bf16[2048,2048]{1,0:T(8,128)(2,1)}), bf16[256,2048]{1,0:T(8,128)(2,1)}) %reduce-scatter.13.cloned.1.call-update) | async-done | bytes 1048592 | tf_op jit(solution)/shard_map/reduce_scatter | solution.py:312
  1319.5 12.5 all-reduce.8
  1332.5 48.7 %reduce-scatter.9.cloned.1.call-done = bf16[256,3,512]{2,0,1:T(8,128)(2,1)} async-done(((bf16[2048,3,512]{2,0,1:T(8,128)(2,1)}), bf16[256,3,512]{2,0,1:T(8,128)(2,1)}) %reduce-scatter.9.cloned.1.call-update) | async-done | bytes 786448 | tf_op jit(solution)/shard_map/reduce_scatter | solution.py:303
  (244 shorter events, 113.4 us)
Async XLA Ops:
  7.2 85.9 %all-gather.14.cloned.1.call-start = ((), (), s32[]{:S(2)}) async-start(), calls=%async_computation.5 | async-start | bytes 5242880 | tf_op jit(solution)/shard_map/all_gather | solution.py:192
  7.9 132.7 %all-gather.16.cloned.1.call-start = ((), (), s32[]{:S(2)}) async-start(), calls=%async_computation.6 | async-start | bytes 7077888 | tf_op jit(solution)/shard_map/all_gather | solution.py:156
  10.3 175.0 %all-gather.18.cloned.1.call-start = ((), (), s32[]{:S(2)}) async-start(), calls=%async_computation.7 | async-start | bytes 2359296 | tf_op jit(solution)/shard_map/all_gather | solution.py:158
  11.0 336.4 %all-reduce.15.cloned.1.call-start = ((), (), s32[]{:S(2)}) async-start(), calls=%async_computation.8 | async-start | bytes 8388608 | tf_op jit(solution)/shard_map/psum | solution.py:200
  22.8 130.3 %copy-start.28 = (f32[8,1,256]{2,1,0:T(1,128)}, f32[8,1,256]{2,1,0:T(1,128)S(1)}, u32[]{:S(2)}) copy-start(f32[8,1,256]{2,1,0:T(1,128)S(1)} %convert_element_type.259) | copy-start | bytes 24580
  31.7 121.3 %copy-start.20 = (f32[8,1,256]{2,1,0:T(1,128)}, f32[8,1,256]{2,1,0:T(1,128)S(1)}, u32[]{:S(2)}) copy-start(f32[8,1,256]{2,1,0:T(1,128)S(1)} %convert_element_type.258) | copy-start | bytes 24580
  95.9 57.2 %copy-start.18 = (f32[1024]{0:T(1024)}, f32[1024]{0:T(1024)S(1)}, u32[]{:S(2)}) copy-start(f32[1024]{0:T(1024)S(1)} %broadcast_multiply_fusion.6) | copy-start | bytes 12292
  99.3 53.8 %copy-start.22 = (f32[1024]{0:T(1024)}, f32[1024]{0:T(1024)S(1)}, u32[]{:S(2)}) copy-start(f32[1024]{0:T(1024)S(1)} %add_rsqrt_fusion.1) | copy-start | bytes 12292
  169.3 3.2 copy-start.14
  180.4 3.2 copy-start.14
  185.2 7.7 copy-start.2
  185.2 7.7 copy-start.6
  185.3 9.7 copy-start.34
  185.3 9.7 copy-start.35
  185.3 9.7 copy-start.36
  185.3 35.5 %copy-start.33 = (bf16[128,2]{0,1:T(2,128)(2,1)S(1)}, bf16[128,2]{0,1:T(2,128)(2,1)}, u32[]{:S(2)}) copy-start(bf16[128,2]{0,1:T(2,128)(2,1)} %param.30) | copy-start | bytes 1540
  192.4 210.0 %all-gather.20.cloned.1.call-start = ((), (), s32[]{:S(2)}) async-start(), calls=%async_computation.9 | async-start | bytes 9437184 | tf_op jit(solution)/shard_map/all_gather | solution.py:162
  193.0 291.6 %all-gather.24.cloned.1.call-start = ((), (), s32[]{:S(2)}) async-start(), calls=%async_computation.11 | async-start | bytes 5242880 | tf_op jit(solution)/shard_map/all_gather | solution.py:193
  193.6 347.3 %all-gather.22.cloned.1.call-start = ((), (), s32[]{:S(2)}) async-start(), calls=%async_computation.10 | async-start | bytes 9437184 | tf_op jit(solution)/shard_map/all_gather | solution.py:164
  194.3 536.0 %all-reduce.17.cloned.1.call-start = ((), (), s32[]{:S(2)}) async-start(), calls=%async_computation.12 | async-start | bytes 8388608 | tf_op jit(solution)/shard_map/psum | solution.py:206
  203.9 198.5 %copy-start.30 = (f32[8,1,256]{2,1,0:T(1,128)}, f32[8,1,256]{2,1,0:T(1,128)S(1)}, u32[]{:S(2)}) copy-start(f32[8,1,256]{2,1,0:T(1,128)S(1)} %convert_element_type.262) | copy-start | bytes 24580
  212.0 524.4 %copy-start.16 = (f32[8,1,256]{2,1,0:T(1,128)}, f32[8,1,256]{2,1,0:T(1,128)S(1)}, u32[]{:S(2)}) copy-start(f32[8,1,256]{2,1,0:T(1,128)S(1)} %convert_element_type.261) | copy-start | bytes 24580
  228.9 311.9 %copy-start.26 = (f32[2048]{0:T(1024)}, f32[2048]{0:T(1024)S(1)}, u32[]{:S(2)}) copy-start(f32[2048]{0:T(1024)S(1)} %reshape.277) | copy-start | bytes 24580
  229.0 507.4 %copy-start.24 = (f32[1024]{0:T(1024)}, f32[1024]{0:T(1024)S(1)}, u32[]{:S(2)}) copy-start(f32[1024]{0:T(1024)S(1)} %fusion.82) | copy-start | bytes 12292
  358.6 5.8 copy-start
  575.2 344.9 %reduce-scatter.17.cloned.1.call-start = ((), (), s32[]{:S(2)}) async-start(), calls=%async_computation.17 | async-start | bytes 36864
  730.4 6.0 copy-start.5
  730.4 7.1 copy-start.10
  745.8 6.5 copy-start.4
  755.7 3.5 copy-start.9
  759.2 3.8 copy-start.7
  767.1 2.5 copy-start.11
  767.1 3.9 copy-start.3
  775.5 3.5 copy-start.9
  779.1 5.1 copy-start.7
  788.2 3.9 copy-start.3
  795.3 10.0 copy-start.27
  797.8 123.8 %reduce-scatter.11.cloned.1.call-start = ((), (), s32[]{:S(2)}) async-start(), calls=%async_computation.14 | async-start | bytes 2359296 | tf_op jit(solution)/shard_map/reduce_scatter | solution.py:309
  805.3 361.3 %all-reduce.19.cloned.1.call-start = ((), (), s32[]{:S(2)}) async-start(), calls=%async_computation.18 | async-start | bytes 16777216 | tf_op jit(solution)/shard_map/psum | solution.py:200
  805.3 16.4 %copy-start.13 = (bf16[2,512,4,128]{3,1,2,0:T(8,128)(2,1)S(1)}, bf16[2,512,4,128]{3,1,2,0:T(8,128)(2,1)}, u32[]{:S(2)}) copy-start(bf16[2,512,4,128]{3,1,2,0:T(8,128)(2,1)} %get-tuple-element.174) | copy-start | bytes 3145732
  843.5 416.4 %reduce-scatter.15.cloned.1.call-start = ((), (), s32[]{:S(2)}) async-start(), calls=%async_computation.16 | async-start | bytes 9437184 | tf_op jit(solution)/shard_map/reduce_scatter | solution.py:318
  864.4 451.8 %reduce-scatter.13.cloned.1.call-start = ((), (), s32[]{:S(2)}) async-start(), calls=%async_computation.15 | async-start | bytes 9437184 | tf_op jit(solution)/shard_map/reduce_scatter | solution.py:312
  880.0 501.2 %reduce-scatter.9.cloned.1.call-start = ((), (), s32[]{:S(2)}) async-start(), calls=%async_computation.13 | async-start | bytes 7077888 | tf_op jit(solution)/shard_map/reduce_scatter | solution.py:303
  880.6 14.2 %copy-start.38 = (u32[32]{0:T(128)S(1)}, u32[32]{0:T(128)}, u32[]{:S(2)}) copy-start(u32[32]{0:T(128)} %constant.157) | copy-start | bytes 388
  880.6 16.1 %copy-start.37 = (bf16[256]{0:T(256)(128)(2,1)S(1)}, bf16[256]{0:T(256)(128)(2,1)}, u32[]{:S(2)}) copy-start(bf16[256]{0:T(256)(128)(2,1)} %param.32) | copy-start | bytes 1540
  894.8 18.3 %copy-start.32 = (bf16[2048]{0:T(1024)(128)(2,1)S(1)}, bf16[2048]{0:T(1024)(128)(2,1)}, u32[]{:S(2)}) copy-start(bf16[2048]{0:T(1024)(128)(2,1)} %get-tuple-element.519) | copy-start | bytes 12292
  1216.1 6.7 copy-start.1
  1216.1 6.7 copy-start.8
  (13 other events, 14.1 us)
Sparse Core Ops, SparseCore 0:
  9.6 83.4 all-gather.13
  95.5 45.0 all-gather.15
  142.5 28.0 all-gather.17
  192.5 154.8 all-reduce.14
  349.1 53.2 all-gather.19
  403.8 80.7 all-gather.23
  486.4 54.3 all-gather.21
  575.3 154.9 all-reduce.16
  797.9 30.3 reduce-scatter.16
  832.0 41.1 reduce-scatter.10
  875.7 290.8 all-reduce.18
  1169.9 71.3 reduce-scatter.14
  1244.7 71.4 reduce-scatter.12
  1319.5 61.6 reduce-scatter.8
where the time goes:
time: 1400 us; the launch traced here: 1390 us
  waiting for transfers between devices  872 us (62%)
  matrix products  195 us (14%)
  blocking collectives  148 us (11%)
  other arithmetic  108 us (8%)
  local copies, waits for them, and re-layouts  41.9 us (3%)
  between operations  17.3 us (1%)
    psum x2, waiting for transfers between devices, branch_total(): lax.psum(jnp.dot(source, weight, preferred_element_type=jnp.float32).asty...  362 us
    psum x1, waiting for transfers between devices, input_total(): lax.psum(contract_cols(source, weight).astype(jnp.bfloat16), 'tensor')  155 us
    all_gather x1, waiting for transfers between devices, shards(): lax.all_gather(cotangent, 'tensor', axis=0, tiled=True)  66.3 us
    dot_general x4, matrix products, contract_rows(): lax.dot_general(left, right, (((0,), (0,)), ((), ())), preferred_element_...  56.6 us
    all_gather x1, waiting for transfers between devices, shards(): lax.all_gather(down_weight, 'dp', axis=1, tiled=True)  56.3 us
    reduce_scatter x1, waiting for transfers between devices, shards(): lax.psum_scatter(up_weight_grad.astype(jnp.bfloat16), 'dp', scatter_dimen...  53.5 us
    all_gather x1, waiting for transfers between devices, shards(): lax.all_gather(tokens, 'tensor', axis=0, tiled=True)  51.9 us
    dot_general x4, matrix products, contract_cols(): lax.dot_general(left, right, (((1,), (1,)), ((), ())), preferred_element_...  50 us
  transfers between devices with their start and end apart: 14, of which 10 were waited for; matrix products, arithmetic and copies ran while one was open for 17% of the time, Pallas kernels for 0%

commit v1 on v0

--- a/solution.py
+++ b/solution.py
@@ -197,9 +197,12 @@
         return lax.dynamic_slice_in_dim(values, own_first, own_rows, 0)
 
     def branch_total(source, weight):
-        return lax.psum(
-            jnp.dot(source, weight, preferred_element_type=jnp.float32).astype(jnp.bfloat16),
-            "tensor",
+        return jnp.sum(
+            lax.all_gather(
+                jnp.dot(source, weight, preferred_element_type=jnp.float32).astype(jnp.bfloat16),
+                "tensor",
+            ),
+            axis=0,
         ).astype(jnp.float32)
 
     def input_total(source, weight):

time: 1400 us -> 1760 us (1.26)
  waiting for transfers between devices: 872 us -> 1200 us
  other arithmetic: 108 us -> 130 us
    all_gather x0 -> x2, waiting for transfers between devices: none -> 536 us  [branch_total(): lax.all_gather(jnp.dot(source, weight, preferred_element_type=jnp.float32...]
    psum x2 -> x0, waiting for transfers between devices: 362 us -> none  [branch_total(): lax.psum(jnp.dot(source, weight, preferred_element_type=jnp.float32).asty...]
    psum x1 -> x2, waiting for transfers between devices: 155 us -> 265 us  [input_total(): lax.psum(contract_cols(source, weight).astype(jnp.bfloat16), 'tensor')]
    reduce_scatter x1, waiting for transfers between devices: 0.01 us -> 72 us  [shards(): lax.psum_scatter(down_weight_grad.astype(jnp.bfloat16), 'dp', scatter_dim...]
    reduce_scatter x1, waiting for transfers between devices: 53.5 us -> 26.8 us  [shards(): lax.psum_scatter(up_weight_grad.astype(jnp.bfloat16), 'dp', scatter_dimen...]
    reduce_sum x0 -> x2, other arithmetic: none -> 24.3 us  [branch_total(): jnp.sum(lax.all_gather(jnp.dot(source, weight, preferred_element_type=jnp...]
  transfers between devices with their start and end apart: 14 -> 15, of which waited for: 10 -> 12; matrix products, arithmetic and copies ran while one was open for 17% -> 13% of each run, Pallas kernels for 0% -> 0%
where the time goes in v1:
time: 1760 us
  waiting for transfers between devices  1200 us (68%)
  matrix products  212 us (12%)
  blocking collectives  144 us (8%)
  other arithmetic  130 us (7%)
  local copies, waits for them, and re-layouts  42.3 us (2%)
  between operations  17.6 us (1%)
    all_gather x2, waiting for transfers between devices, branch_total(): lax.all_gather(jnp.dot(source, weight, preferred_element_type=jnp.float32...  536 us
    psum x2, waiting for transfers between devices, input_total(): lax.psum(contract_cols(source, weight).astype(jnp.bfloat16), 'tensor')  265 us
    reduce_scatter x1, waiting for transfers between devices, shards(): lax.psum_scatter(down_weight_grad.astype(jnp.bfloat16), 'dp', scatter_dim...  72 us
    all_gather x1, waiting for transfers between devices, shards(): lax.all_gather(cotangent, 'tensor', axis=0, tiled=True)  66.6 us
    reduce_scatter x1, waiting for transfers between devices, shards(): lax.psum_scatter(qkv_weight_grad.astype(jnp.bfloat16), 'dp', scatter_dime...  62.2 us
    all_gather x1, waiting for transfers between devices, shards(): lax.all_gather(down_weight, 'dp', axis=1, tiled=True)  56.3 us
    dot_general x4, matrix products, contract_rows(): lax.dot_general(left, right, (((0,), (0,)), ((), ())), preferred_element_...  55.2 us
    all_gather x1, waiting for transfers between devices, shards(): lax.all_gather(tokens, 'tensor', axis=0, tiled=True)  51.9 us
  transfers between devices with their start and end apart: 15, of which 12 were waited for; matrix products, arithmetic and copies ran while one was open for 13% of the time, Pallas kernels for 0%

profile of v1, /device:TPU:0, one launch (start us, length us, event | category | flops | bytes accessed | tf_op | source)
XLA Modules:
  0.0 1755.9 jit_solution(9753565067106414055)
XLA Ops:
  11.9 10.7 all_gather.58
  23.7 8.9 all-gather.2
  33.2 7.9 all-gather.3
  41.2 51.9 %all-gather.18.cloned.1.call-done = bf16[1024,2048]{1,0:T(8,128)(2,1)} async-done(((bf16[256,2048]{1,0:T(8,128)(2,1)}), bf16[1024,2048]{1,0:T(8,128)(2,1)}) %all-gather.18.cloned.1.call-update) | async-done | bytes 4194320 | tf_op jit(solution)/shard_map/all_gather | solution.py:192
  99.3 41.3 %all-gather.20.cloned.1.call-done = bf16[2048,3,512]{0,2,1:T(8,128)(2,1)} async-done(((bf16[256,3,512]{0,2,1:T(8,128)(2,1)}), bf16[2048,3,512]{0,2,1:T(8,128)(2,1)}) %all-gather.20.cloned.1.call-update) | async-done | bytes 6291472 | tf_op jit(solution)/shard_map/all_gather | solution.py:156
  140.6 12.6 add_convert_fusion.2
  159.7 22.2 %while.50 = (s32[]{:T(128)}, bf16[2,512,4,128]{3,2,1,0:T(4,128)(2,1)}, f32[2,4,512]{2,1,0:T(4,128)S(1)}, s32[2]{0:T(128)S(1)}, s32[]{:T(128)}, /*index=5*/bf16[1...) while((s32[]{:T(128)}, ...), condition=%wide.region_5.6_spmd.clone.clone, body=%wide.region_2.5_spmd.clone.clone.sunk | while | flops 1100217856 | bytes 31529664 | solution.py:68
  182.0 6.9 convolution_convert_fusion.6
  191.5 8.9 all-gather.4
  200.4 8.0 all-gather.5
  208.5 8.9 all-gather.6
  217.4 7.9 all-gather.7
  225.5 250.3 %all-gather.30.cloned.1.call-done = bf16[4096,2048]{1,0:T(8,128)(2,1)} async-done(((bf16[1024,2048]{1,0:T(8,128)(2,1)}), bf16[4096,2048]{1,0:T(8,128)(2,1)}) %all-gather.30.cloned.1.call-update) | async-done | bytes 16777232 | tf_op jit(solution)/shard_map/all_gather | solution.py:201
  475.8 12.3 reduce_sum.258
  488.1 10.6 fusion.84
  509.2 20.8 %all-gather.24.cloned.1.call-done = bf16[2048,2048]{1,0:T(8,128)(2,1)} async-done(((bf16[256,2048]{1,0:T(8,128)(2,1)}), bf16[2048,2048]{1,0:T(8,128)(2,1)}) %all-gather.24.cloned.1.call-update) | async-done | bytes 8388624 | tf_op jit(solution)/shard_map/all_gather | solution.py:162
  530.0 15.6 fusion.69
  545.6 66.6 %all-gather.28.cloned.1.call-done = bf16[1024,2048]{1,0:T(8,128)(2,1)} async-done(((bf16[256,2048]{1,0:T(8,128)(2,1)}), bf16[1024,2048]{1,0:T(8,128)(2,1)}) %all-gather.28.cloned.1.call-update) | async-done | bytes 4194320 | tf_op jit(solution)/shard_map/all_gather | solution.py:193
  612.2 56.3 %all-gather.26.cloned.1.call-done = bf16[2048,2048]{1,0:T(8,128)(2,1)} async-done(((bf16[2048,256]{1,0:T(8,128)(2,1)}), bf16[2048,2048]{1,0:T(8,128)(2,1)}) %all-gather.26.cloned.1.call-update) | async-done | bytes 8388624 | tf_op jit(solution)/shard_map/all_gather | solution.py:164
  668.4 19.3 %fusion.87 = (bf16[2048]{0:T(1024)(128)(2,1)}, bf16[1024,2048]{1,0:T(8,128)(2,1)S(1)}) fusion(f32[1024,2048]{1,0:T(8,128)} %fusion.69, f32[2048]{0:T(1024)S(1)} %reshape.277, bf16[2048,2048]{1,0:T(8,128)(2,1)} %all-gather.26.cloned.1.call-done, f32[1024]{0:T(1024)S(1)} %fusion.82, bf16[1024,2048]{1,0:T(8,128)(2,1)} %all-gather.28.cloned.1.call-done), kind=kOutput, calls=%fused_computation.167 | convolution fusion | flops 8642361344 | bytes 25182208 | tf_op jit(solution)/shard_map/dot_general | solution.py:37
  689.7 12.6 convolution_convert_fusion.4
  702.5 155.1 %all-reduce.13.cloned.1.call-done = bf16[1024,2048]{1,0:T(8,128)(2,1)} async-done(((bf16[1024,2048]{1,0:T(8,128)(2,1)}), bf16[1024,2048]{1,0:T(8,128)(2,1)}) %all-reduce.13.cloned.1.call-update) | async-done | bytes 4194320 | tf_op jit(solution)/shard_map/psum | solution.py:209
  857.5 6.0 multiply_reduce_fusion.5
  864.6 8.3 convert_multiply_fusion
  872.9 6.5 fusion.66
  879.4 66.1 %while.51 = (s32[]{:T(128)}, f32[1024,4,128]{0,2,1:T(8,128)S(1)}, f32[1024,4,128]{0,2,1:T(8,128)}, bf16[2,512,4,128]{3,1,2,0:T(8,128)(2,1)}, s32[2]{0:T(128)S(1)...) while((s32[]{:T(128)}, f32[1024,4,128]{0,2,1:T(8,128)S(1)}, ...), condition=%wide.region_15.16_spmd.clone.clone, body=%wide.region_13.15_spmd.clone.clone.sunk | while | flops 2720005632 | bytes 171506224 | solution.py:113
  881.1 5.5 fusion.140
  889.6 7.7 multiply_reduce_fusion.8
  913.3 5.5 fusion.140
  921.9 7.7 multiply_reduce_fusion.8
  950.2 7.4 convolution_convert_fusion.7
  966.4 11.3 convolution_convert_fusion.3
  977.8 14.6 convolution_convert_fusion.1
  993.1 20.2 %convolution_convert_fusion = bf16[2048,2048]{1,0:T(8,128)(2,1)} fusion(bf16[1024,2048]{1,0:T(8,128)(2,1)} %all-gather.28.cloned.1.call-done, f32[1024]{0:T(1024)S(1)} %copy-done.23, f32[1024,2048]{1,0:T(8,128)} %fusion.69, f32[2048]{0:T(1024)S(1)} %copy-done.25), kind=kOutput, calls=%fused_computation.77 | convolution fusion | flops 8621391872 | bytes 20983808 | tf_op jit(solution)/shard_map/dot_general | solution.py:31
  1015.2 13.1 convolution_convert_fusion.2
  1028.6 16.2 convolution_convert_fusion.5
  1044.9 8.7 all-gather.8
  1056.3 6.5 convert_element_type.201
  1073.1 109.6 %all-reduce.15.cloned.1.call-done = bf16[1024,2048]{1,0:T(8,128)(2,1)} async-done(((bf16[1024,2048]{1,0:T(8,128)(2,1)}), bf16[1024,2048]{1,0:T(8,128)(2,1)}) %all-reduce.15.cloned.1.call-update) | async-done | bytes 4194320 | tf_op jit(solution)/shard_map/psum | solution.py:209
  1193.6 24.4 %all-reduce.9 = (bf16[2048]{0:T(1024)(128)(2,1)S(1)}, bf16[2048]{0:T(1024)(128)(2,1)S(1)}, bf16[2048]{0:T(1024)(128)(2,1)S(1)}, bf16[2048]{0:T(1024)(128)(2,1)S(...) all-reduce(bf16[2048]{0:T(1024)(128)(2,1)S(1)} %get-tuple-element.5, ...), channel_id=4, replica_groups=mesh['dp'=8,'tensor'=4] {'dp'}, use_global_device_ids=true, to_apply=%region_20.21.clone | all-reduce | flops 14336 | bytes 57344
  1219.2 10.7 all-reduce.8
  1229.9 26.8 %reduce-scatter.13.cloned.1.call-done = bf16[256,2048]{1,0:T(8,128)(2,1)} async-done(((bf16[2048,2048]{1,0:T(8,128)(2,1)}), bf16[256,2048]{1,0:T(8,128)(2,1)}) %reduce-scatter.13.cloned.1.call-update) | async-done | bytes 1048592 | tf_op jit(solution)/shard_map/reduce_scatter | solution.py:315
  1259.5 72.0 %reduce-scatter.15.cloned.1.call-done = bf16[2048,256]{1,0:T(8,128)(2,1)} async-done(((bf16[2048,2048]{1,0:T(8,128)(2,1)}), bf16[2048,256]{1,0:T(8,128)(2,1)}) %reduce-scatter.15.cloned.1.call-update) | async-done | bytes 1048592 | tf_op jit(solution)/shard_map/reduce_scatter | solution.py:321
  1334.2 62.2 %reduce-scatter.9.cloned.1.call-done = bf16[256,3,512]{2,0,1:T(8,128)(2,1)} async-done(((bf16[2048,3,512]{2,0,1:T(8,128)(2,1)}), bf16[256,3,512]{2,0,1:T(8,128)(2,1)}) %reduce-scatter.9.cloned.1.call-update) | async-done | bytes 786448 | tf_op jit(solution)/shard_map/reduce_scatter | solution.py:306
  1398.9 285.7 %all-gather.32.cloned.1.call-done = bf16[4096,2048]{1,0:T(8,128)(2,1)} async-done(((bf16[1024,2048]{1,0:T(8,128)(2,1)}), bf16[4096,2048]{1,0:T(8,128)(2,1)}) %all-gather.32.cloned.1.call-update) | async-done | bytes 16777232 | tf_op jit(solution)/shard_map/all_gather | solution.py:201
  1684.6 12.0 reduce_sum.261
  1700.0 5.7 fusion.52
  1705.7 38.8 %all-reduce.7 = (f32[1]{0:T(128)}, f32[1]{0:T(128)}, f32[1]{0:T(128)}, f32[1]{0:T(128)}, f32[1]{0:T(128)}, /*index=5*/f32[]{:T(128)}) all-reduce(f32[1]{0:T(128)} %bitcast.27, f32[1]{0:T(128)} %bitcast.28, f32[1]{0:T(128)} %bitcast.29, f32[1]{0:T(128)} %bitcast.30, ...), channel_id=1, replica_groups=mesh['dp'=8,'tensor'=4] {'dp','tensor'}, use_global_device_ids=true, to_apply=%region_47.48 | all-reduce | flops 6 | bytes 48 | tf_op jit(solution)/shard_map/psum | solution.py:218
  (255 shorter events, 144.2 us)
Async XLA Ops:
  7.2 85.9 %all-gather.18.cloned.1.call-start = ((), (), s32[]{:S(2)}) async-start(), calls=%async_computation.5 | async-start | bytes 5242880 | tf_op jit(solution)/shard_map/all_gather | solution.py:192
  7.9 132.7 %all-gather.20.cloned.1.call-start = ((), (), s32[]{:S(2)}) async-start(), calls=%async_computation.6 | async-start | bytes 7077888 | tf_op jit(solution)/shard_map/all_gather | solution.py:156
  10.3 171.6 %all-gather.22.cloned.1.call-start = ((), (), s32[]{:S(2)}) async-start(), calls=%async_computation.7 | async-start | bytes 2359296 | tf_op jit(solution)/shard_map/all_gather | solution.py:158
  11.0 464.8 %all-gather.30.cloned.1.call-start = ((), (), s32[]{:S(2)}) async-start(), calls=%async_computation.17 | async-start | bytes 20971520 | tf_op jit(solution)/shard_map/all_gather | solution.py:201
  32.6 108.1 %copy-start.18 = (f32[8,1,256]{2,1,0:T(1,128)}, f32[8,1,256]{2,1,0:T(1,128)S(1)}, u32[]{:S(2)}) copy-start(f32[8,1,256]{2,1,0:T(1,128)S(1)} %convert_element_type.262) | copy-start | bytes 24580
  41.2 99.4 %copy-start.26 = (f32[8,1,256]{2,1,0:T(1,128)}, f32[8,1,256]{2,1,0:T(1,128)S(1)}, u32[]{:S(2)}) copy-start(f32[8,1,256]{2,1,0:T(1,128)S(1)} %convert_element_type.263) | copy-start | bytes 24580
  95.9 44.7 %copy-start.16 = (f32[1024]{0:T(1024)}, f32[1024]{0:T(1024)S(1)}, u32[]{:S(2)}) copy-start(f32[1024]{0:T(1024)S(1)} %broadcast_multiply_fusion.6) | copy-start | bytes 12292
  99.3 41.3 %copy-start.20 = (f32[1024]{0:T(1024)}, f32[1024]{0:T(1024)S(1)}, u32[]{:S(2)}) copy-start(f32[1024]{0:T(1024)S(1)} %add_rsqrt_fusion.1) | copy-start | bytes 12292
  181.9 7.6 copy-start.5
  181.9 7.6 copy-start.8
  181.9 9.6 copy-start.32
  181.9 18.5 %copy-start.33 = (bf16[256]{0:T(256)(128)(2,1)S(1)}, bf16[256]{0:T(256)(128)(2,1)}, u32[]{:S(2)}) copy-start(bf16[256]{0:T(256)(128)(2,1)} %param.27) | copy-start | bytes 1540
  181.9 26.5 %copy-start.34 = (bf16[256]{0:T(256)(128)(2,1)S(1)}, bf16[256]{0:T(256)(128)(2,1)}, u32[]{:S(2)}) copy-start(bf16[256]{0:T(256)(128)(2,1)} %param.28) | copy-start | bytes 1540
  181.9 35.4 %copy-start.31 = (bf16[128,2]{0,1:T(2,128)(2,1)S(1)}, bf16[128,2]{0,1:T(2,128)(2,1)}, u32[]{:S(2)}) copy-start(bf16[128,2]{0,1:T(2,128)(2,1)} %param.30) | copy-start | bytes 1540
  188.9 341.1 %all-gather.24.cloned.1.call-start = ((), (), s32[]{:S(2)}) async-start(), calls=%async_computation.8 | async-start | bytes 9437184 | tf_op jit(solution)/shard_map/all_gather | solution.py:162
  189.5 422.7 %all-gather.28.cloned.1.call-start = ((), (), s32[]{:S(2)}) async-start(), calls=%async_computation.10 | async-start | bytes 5242880 | tf_op jit(solution)/shard_map/all_gather | solution.py:193
  190.1 478.4 %all-gather.26.cloned.1.call-start = ((), (), s32[]{:S(2)}) async-start(), calls=%async_computation.9 | async-start | bytes 9437184 | tf_op jit(solution)/shard_map/all_gather | solution.py:164
  190.8 666.7 %all-reduce.13.cloned.1.call-start = ((), (), s32[]{:S(2)}) async-start(), calls=%async_computation.11 | async-start | bytes 8388608 | tf_op jit(solution)/shard_map/psum | solution.py:209
  217.4 312.6 %copy-start.28 = (f32[8,1,256]{2,1,0:T(1,128)}, f32[8,1,256]{2,1,0:T(1,128)S(1)}, u32[]{:S(2)}) copy-start(f32[8,1,256]{2,1,0:T(1,128)S(1)} %convert_element_type.266) | copy-start | bytes 24580
  225.4 443.0 %copy-start.24 = (f32[2048]{0:T(1024)}, f32[2048]{0:T(1024)S(1)}, u32[]{:S(2)}) copy-start(f32[2048]{0:T(1024)S(1)} %reshape.277) | copy-start | bytes 24580
  225.4 638.1 %copy-start.22 = (f32[1024]{0:T(1024)}, f32[1024]{0:T(1024)S(1)}, u32[]{:S(2)}) copy-start(f32[1024]{0:T(1024)S(1)} %fusion.82) | copy-start | bytes 12292
  498.7 6.5 copy-start.2
  702.4 367.5 %reduce-scatter.17.cloned.1.call-start = ((), (), s32[]{:S(2)}) async-start(), calls=%async_computation.19 | async-start | bytes 36864
  857.5 7.1 copy-start.12
  872.9 6.5 copy-start.6
  889.2 8.2 slice-start
  889.6 7.7 copy-start.3
  889.6 7.7 slice-start.1
  901.1 6.5 copy-start
  901.1 6.8 copy-start.4
  901.1 7.1 copy-start.11
  921.4 8.2 slice-start
  921.9 7.7 copy-start.3
  921.9 7.7 slice-start.1
  933.3 6.5 copy-start
  933.4 6.8 copy-start.4
  933.4 7.1 copy-start.11
  947.3 12.7 copy-start.10
  950.0 121.3 %reduce-scatter.11.cloned.1.call-start = ((), (), s32[]{:S(2)}) async-start(), calls=%async_computation.14 | async-start | bytes 2359296 | tf_op jit(solution)/shard_map/reduce_scatter | solution.py:312
  957.7 225.1 %all-reduce.15.cloned.1.call-start = ((), (), s32[]{:S(2)}) async-start(), calls=%async_computation.12 | async-start | bytes 8388608 | tf_op jit(solution)/shard_map/psum | solution.py:209
  966.4 11.4 copy-start.29
  977.7 279.0 %reduce-scatter.13.cloned.1.call-start = ((), (), s32[]{:S(2)}) async-start(), calls=%async_computation.15 | async-start | bytes 9437184 | tf_op jit(solution)/shard_map/reduce_scatter | solution.py:315
  992.4 339.1 %reduce-scatter.15.cloned.1.call-start = ((), (), s32[]{:S(2)}) async-start(), calls=%async_computation.16 | async-start | bytes 9437184 | tf_op jit(solution)/shard_map/reduce_scatter | solution.py:321
  1013.3 383.1 %reduce-scatter.9.cloned.1.call-start = ((), (), s32[]{:S(2)}) async-start(), calls=%async_computation.13 | async-start | bytes 7077888 | tf_op jit(solution)/shard_map/reduce_scatter | solution.py:306
  1028.3 16.6 copy-start.35
  1028.3 25.3 %copy-start.36 = (u32[32]{0:T(128)S(1)}, u32[32]{0:T(128)}, u32[]{:S(2)}) copy-start(u32[32]{0:T(128)} %constant.159) | copy-start | bytes 388
  1028.3 656.3 %all-gather.32.cloned.1.call-start = ((), (), s32[]{:S(2)}) async-start(), calls=%async_computation.18 | async-start | bytes 20971520 | tf_op jit(solution)/shard_map/all_gather | solution.py:201
  1044.8 17.9 %copy-start.30 = (bf16[2048]{0:T(1024)(128)(2,1)S(1)}, bf16[2048]{0:T(1024)(128)(2,1)}, u32[]{:S(2)}) copy-start(bf16[2048]{0:T(1024)(128)(2,1)} %get-tuple-element.517) | copy-start | bytes 12292
  (16 other events, 41.9 us)
Sparse Core Ops, SparseCore 0:
  9.6 83.4 all-gather.17
  95.5 45.0 all-gather.19
  142.5 28.0 all-gather.21
  189.0 286.7 all-gather.29
  477.5 52.4 all-gather.23
  531.4 80.7 all-gather.27
  614.1 54.3 all-gather.25
  702.5 154.9 all-reduce.12
  950.1 30.2 reduce-scatter.16
  984.2 41.1 reduce-scatter.10
  1027.7 154.9 all-reduce.14
  1186.0 70.6 reduce-scatter.12
  1260.2 71.2 reduce-scatter.14
  1334.7 61.6 reduce-scatter.8
  1397.8 286.7 all-gather.31
